TPU v7x, 128 devices: a whole 4x4x4 slice. The times are simulated.
128 devices in a mesh: rows: 16 (over z_lo, x, core), batch: 8 (over z_hi, y).
Axes of the slice: x: 4, y: 4, z: 4 (z_hi: 2, z_lo: 2; z = z_hi * 2 + z_lo), core: 2. Of those that a mesh axis runs over, the one named last changes fastest.
Arguments:
- bases: bfloat16 [49152, 2048], P('rows', 'batch'), may hold values from -30 to 30
- start: float32 [2048, 512], P('batch'), may hold values from -6 to 6
Outputs:
- modes: bfloat16 [49152, 512], P(('rows', 'batch'))
All inputs are finite; a program needn't handle non-finite values.
Results may differ from a plain program's by a relative error of at most 0.0041.
Values may be sent and summed in bfloat16 or wider, within the bound.
A program may use at most 128 MiB of HBM per device.

v0:
```python
import jax
import jax.numpy as jnp
from jax import lax
from jax.sharding import PartitionSpec as P

ITERS = 2


def inner_cols(left, right):
    return lax.dot_general(
        left, right, (((0,), (0,)), ((), ())), preferred_element_type=jnp.float32
    )


def on_device(bases, start):
    basis_width = bases.shape[1]
    group_count = lax.axis_size("batch")
    all_columns = basis_width * group_count
    energy = lax.psum(jnp.sum(jnp.square(bases.astype(jnp.float32))), ("rows", "batch"))
    diag_mean = energy / all_columns
    partial_value = inner_cols(bases, lax.all_gather(bases, "batch", axis=1, tiled=True))
    gram_rows = lax.psum(partial_value, "rows")
    q_own = start
    for iteration in range(ITERS):
        q_full = lax.all_gather(q_own, "batch", axis=0, tiled=True)
        lifted = jnp.dot(gram_rows, q_full, precision=lax.Precision.HIGHEST) / diag_mean + q_own
        local_correlation = lax.dot_general(
            lifted, lifted, (((0,), (0,)), ((), ())), precision=lax.Precision.HIGHEST
        )
        correlation = lax.psum(local_correlation, "batch")
        factor = jnp.linalg.cholesky(correlation)
        q_own = jax.scipy.linalg.solve_triangular(factor, lifted.T, lower=True).T
    q_low = q_own.astype(jnp.bfloat16)
    modes = lax.psum_scatter(
        jnp.dot(bases, q_low, preferred_element_type=jnp.float32),
        "batch",
        scatter_dimension=0,
        tiled=True,
    )
    return modes.astype(jnp.bfloat16)


def solution(mesh):
    in_specs = (P("rows", "batch"), P("batch", None))
    out_specs = P(("rows", "batch"), None)
    return jax.shard_map(
        on_device, mesh=mesh, in_specs=in_specs, out_specs=out_specs, check_vma=False
    )
```

profile of v0, /device:TPU:0, one launch (start us, length us, event | category | flops | bytes accessed | tf_op | source)
XLA Modules:
  0.0 1044.4 jit_solution(2930456255555356268)
XLA Ops:
  8.1 166.4 %all-gather.4.cloned.1.call-done = bf16[3072,2048]{1,0:T(8,128)(2,1)} async-done(((bf16[3072,256]{1,0:T(8,128)(2,1)}), bf16[3072,2048]{1,0:T(8,128)(2,1)}) %all-gather.4.cloned.1.call-update) | async-done | bytes 12582928 | tf_op jit(solution)/shard_map/all_gather | solution.py:21
  183.7 78.1 %psum.29 = f32[]{:T(128)} all-reduce(f32[]{:T(128)} %multiply_reduce_fusion), channel_id=1, replica_groups=mesh['rows'=16,'batch'=8] {'rows','batch'}, use_global_device_ids=true, to_apply=%region_2.0 | all-reduce | flops 1 | bytes 8 | tf_op jit(solution)/shard_map/psum | solution.py:19
  262.5 108.6 %all-reduce.5.cloned.1.call-done = f32[256,2048]{1,0:T(8,128)} async-done(((f32[256,2048]{1,0:T(8,128)}), f32[256,2048]{1,0:T(8,128)}) %all-reduce.5.cloned.1.call-update) | async-done | bytes 2097168 | tf_op jit(solution)/shard_map/psum | solution.py:22
  379.9 88.5 %all-reduce.7.cloned.1.call-done = f32[512,512]{0,1:T(8,128)} async-done(((f32[512,512]{0,1:T(8,128)}), f32[512,512]{0,1:T(8,128)}) %all-reduce.7.cloned.1.call-update) | async-done | bytes 1048592 | tf_op jit(solution)/shard_map/psum | solution.py:30
  473.6 11.7 %cholesky.286 = f32[128,128]{1,0:T(8,128)S(1)} custom-call(f32[128,128]{1,0:T(8,128)S(1)} %cholesky.426), custom_call_target="Cholesky" | custom-call | tf_op jit(solution)/shard_map/jit(cholesky)/cholesky | solution.py:31
  485.4 9.8 custom-call.27
  497.8 11.7 %cholesky.305 = f32[128,128]{1,0:T(8,128)S(1)} custom-call(f32[128,128]{1,0:T(8,128)S(1)} %cholesky.430), custom_call_target="Cholesky" | custom-call | tf_op jit(solution)/shard_map/jit(cholesky)/cholesky | solution.py:31
  509.6 10.0 custom-call.28
  521.1 11.7 %cholesky.326 = f32[128,128]{1,0:T(8,128)S(1)} custom-call(f32[128,128]{1,0:T(8,128)S(1)} %cholesky.435), custom_call_target="Cholesky" | custom-call | tf_op jit(solution)/shard_map/jit(cholesky)/cholesky | solution.py:31
  544.8 11.7 %cholesky.343 = f32[128,128]{1,0:T(8,128)S(1)} custom-call(f32[128,128]{1,0:T(8,128)S(1)} %convolution_subtract_fusion.11), custom_call_target="Cholesky" | custom-call | tf_op jit(solution)/shard_map/jit(cholesky)/cholesky | solution.py:31
  561.8 11.7 %while.4 = (s32[]{:T(128)}, f32[512,512]{1,0:T(8,128)}, s32[4,2]{0,1:T(2,128)S(1)}, f32[4,128,128]{2,1,0:T(8,128)S(1)}, s32[]{:T(128)}) while((s32[]{:T(128)}, f32[512,512]{1,0:T(8,128)}, s32[4,2]{0,1:T(2,128)S(1)}, f32[4,128,128]{2,1,0:T(8,128)S(1)}, s32[]{:T(128)}) %tuple.52), condition=%wide.while_cond, body=%wide.while_body.sunk | while | flops 2 | bytes 131181 | solution.py:32
  573.5 39.3 %custom-call.30 = f32[4,128,128]{1,2,0:T(8,128)S(1)} custom-call(f32[4,128,128]{2,1,0:T(8,128)S(1)} %get-tuple-element.21), custom_call_target="InvertDiagBlocksLowerTriangular" | custom-call | tf_op jit(solution)/shard_map/jit(_solve_triangular)/triangular_solve | solution.py:32
  619.7 69.7 %all-gather.8.cloned.1.call-done = f32[2048,512]{1,0:T(8,128)} async-done(((f32[256,512]{1,0:T(8,128)}), f32[2048,512]{1,0:T(8,128)}) %all-gather.8.cloned.1.call-update) | async-done | bytes 4194320 | tf_op jit(solution)/shard_map/all_gather | solution.py:25
  698.3 85.3 %all-reduce.9.cloned.1.call-done = f32[512,512]{0,1:T(8,128)} async-done(((f32[512,512]{0,1:T(8,128)}), f32[512,512]{0,1:T(8,128)}) %all-reduce.9.cloned.1.call-update) | async-done | bytes 1048592 | tf_op jit(solution)/shard_map/psum | solution.py:30
  788.8 11.7 %cholesky.358 = f32[128,128]{1,0:T(8,128)S(1)} custom-call(f32[128,128]{1,0:T(8,128)S(1)} %cholesky.439), custom_call_target="Cholesky" | custom-call | tf_op jit(solution)/shard_map/jit(cholesky)/cholesky | solution.py:31
  800.7 9.8 custom-call.31
  813.1 11.7 %cholesky.377 = f32[128,128]{1,0:T(8,128)S(1)} custom-call(f32[128,128]{1,0:T(8,128)S(1)} %cholesky.443), custom_call_target="Cholesky" | custom-call | tf_op jit(solution)/shard_map/jit(cholesky)/cholesky | solution.py:31
  826.2 9.9 custom-call.32
  837.7 11.7 %cholesky.398 = f32[128,128]{1,0:T(8,128)S(1)} custom-call(f32[128,128]{1,0:T(8,128)S(1)} %cholesky.448), custom_call_target="Cholesky" | custom-call | tf_op jit(solution)/shard_map/jit(cholesky)/cholesky | solution.py:31
  850.1 9.8 custom-call.33
  861.3 11.7 %cholesky.415 = f32[128,128]{1,0:T(8,128)S(1)} custom-call(f32[128,128]{1,0:T(8,128)S(1)} %convolution_subtract_fusion.10), custom_call_target="Cholesky" | custom-call | tf_op jit(solution)/shard_map/jit(cholesky)/cholesky | solution.py:31
  877.7 11.7 %while.5 = (s32[]{:T(128)}, f32[512,512]{1,0:T(8,128)}, s32[4,2]{0,1:T(2,128)S(1)}, f32[4,128,128]{2,1,0:T(8,128)S(1)}, s32[]{:T(128)}) while((s32[]{:T(128)}, f32[512,512]{1,0:T(8,128)}, s32[4,2]{0,1:T(2,128)S(1)}, f32[4,128,128]{2,1,0:T(8,128)S(1)}, s32[]{:T(128)}) %tuple.72), condition=%wide.while_cond.clone, body=%wide.while_body.clone.sunk | while | flops 2 | bytes 131181 | solution.py:32
  889.4 39.3 %custom-call.34 = f32[4,128,128]{1,2,0:T(8,128)S(1)} custom-call(f32[4,128,128]{2,1,0:T(8,128)S(1)} %get-tuple-element.22), custom_call_target="InvertDiagBlocksLowerTriangular" | custom-call | tf_op jit(solution)/shard_map/jit(_solve_triangular)/triangular_solve | solution.py:32
  938.2 97.0 %reduce-scatter.2.cloned.1.call-done = f32[384,512]{0,1:T(8,128)} async-done(((f32[3072,512]{0,1:T(8,128)}), f32[384,512]{0,1:T(8,128)}) %reduce-scatter.2.cloned.1.call-update) | async-done | bytes 786448 | tf_op jit(solution)/shard_map/reduce_scatter | solution.py:34
  (124 shorter events, 109.2 us)
Async XLA Ops:
  6.5 167.9 %copy-start = (bf16[3072,256]{1,0:T(8,128)(2,1)S(1)}, bf16[3072,256]{1,0:T(8,128)(2,1)}, u32[]{:S(2)}) copy-start(bf16[3072,256]{1,0:T(8,128)(2,1)} %param.5) | copy-start | bytes 4718596
  6.5 167.9 %all-gather.4.cloned.1.call-start = ((), (), s32[]{:S(2)}) async-start(), calls=%async_computation.1 | async-start | bytes 14155776 | tf_op jit(solution)/shard_map/all_gather | solution.py:21
  7.3 255.2 %all-gather.6.cloned.1.call-start = ((), (), s32[]{:S(2)}) async-start(), calls=%async_computation.3 | async-start | bytes 4718592 | tf_op jit(solution)/shard_map/all_gather | solution.py:25
  8.0 363.1 %all-reduce.5.cloned.1.call-start = ((), (), s32[]{:S(2)}) async-start(), calls=%async_computation.2 | async-start | bytes 4194304 | tf_op jit(solution)/shard_map/psum | solution.py:22
  182.2 188.8 %copy-start.5 = (f32[256,512]{1,0:T(8,128)S(1)}, f32[256,512]{1,0:T(8,128)}, u32[]{:S(2)}) copy-start(f32[256,512]{1,0:T(8,128)} %param.6) | copy-start | bytes 1572868
  182.3 286.2 %all-reduce.7.cloned.1.call-start = ((), (), s32[]{:S(2)}) async-start(), calls=%async_computation.4 | async-start | bytes 2097152 | tf_op jit(solution)/shard_map/psum | solution.py:30
  379.4 310.0 %all-gather.8.cloned.1.call-start = ((), (), s32[]{:S(2)}) async-start(), calls=%async_computation.5 | async-start | bytes 4718592 | tf_op jit(solution)/shard_map/all_gather | solution.py:25
  468.5 2.7 copy-start.1
  472.6 1.0 copy-start.4
  619.7 164.0 %all-reduce.9.cloned.1.call-start = ((), (), s32[]{:S(2)}) async-start(), calls=%async_computation.6 | async-start | bytes 2097152 | tf_op jit(solution)/shard_map/psum | solution.py:30
  697.9 337.3 %reduce-scatter.2.cloned.1.call-start = ((), (), s32[]{:S(2)}) async-start(), calls=%async_computation.7 | async-start | bytes 7077888 | tf_op jit(solution)/shard_map/reduce_scatter | solution.py:34
  783.7 2.7 copy-start.2
  787.8 1.0 copy-start.3
Sparse Core Ops, SparseCore 0:
  9.5 164.8 all-gather.3
  176.7 70.8 all-gather.5
  250.1 120.8 all-reduce.4
  379.5 88.8 all-reduce.6
  619.8 69.5 all-gather.7
  698.0 85.6 all-reduce.8
  938.4 96.8 reduce-scatter.1
where the time goes:
time: 1050 us; the launch traced here: 1040 us
  waiting for transfers between devices  617 us (59%)
  other arithmetic  246 us (23%)
  blocking collectives  78.1 us (7%)
  matrix products  50.6 us (5%)
  local copies, waits for them, and re-layouts  32.1 us (3%)
  between operations  19.8 us (2%)
    psum x2, waiting for transfers between devices, on_device(): correlation = lax.psum(local_correlation, 'batch')  174 us
    all_gather x1, waiting for transfers between devices, on_device(): lax.all_gather(bases, 'batch', axis=1, tiled=True)  166 us
    another operation x29, other arithmetic, on_device(): factor = jnp.linalg.cholesky(correlation)  158 us
    psum x1, waiting for transfers between devices, on_device(): gram_rows = lax.psum(partial_value, 'rows')  109 us
    reduce_scatter x1, waiting for transfers between devices, on_device(): lax.psum_scatter(jnp.dot(bases, q_low, preferred_element_type=jnp.float32...  97 us
    another operation x5, other arithmetic, on_device(): q_own = jax.scipy.linalg.solve_triangular(factor, lifted.T, lower=True).T  81.3 us
    psum x1, blocking collectives, on_device(): lax.psum(jnp.sum(jnp.square(bases.astype(jnp.float32))), ('rows', 'batch'))  78.1 us
    all_gather x2, waiting for transfers between devices, on_device(): q_full = lax.all_gather(q_own, 'batch', axis=0, tiled=True)  69.7 us
  transfers between devices with their start and end apart: 7, of which 6 were waited for; matrix products, arithmetic and copies ran while one was open for 1% of the time, Pallas kernels for 0%

commit v1 on v0

--- a/solution.py
+++ b/solution.py
@@ -27,7 +27,7 @@
         local_correlation = lax.dot_general(
             lifted, lifted, (((0,), (0,)), ((), ())), precision=lax.Precision.HIGHEST
         )
-        correlation = lax.psum(local_correlation, "batch")
+        correlation = jnp.sum(lax.all_gather(local_correlation, "batch"), axis=0)
         factor = jnp.linalg.cholesky(correlation)
         q_own = jax.scipy.linalg.solve_triangular(factor, lifted.T, lower=True).T
     q_low = q_own.astype(jnp.bfloat16)

time: 1050 us -> 1100 us (1.048)
  waiting for transfers between devices: 617 us -> 658 us
    all_gather x0 -> x2, waiting for transfers between devices: none -> 215 us  [on_device(): correlation = jnp.sum(lax.all_gather(local_correlation, 'batch'), axis=0)]
    psum x2 -> x0, waiting for transfers between devices: 174 us -> none  [on_device(): correlation = lax.psum(local_correlation, 'batch')]
where the time goes in v1:
time: 1100 us; the launch traced here: 1090 us
  waiting for transfers between devices  658 us (60%)
  other arithmetic  254 us (23%)
  blocking collectives  78.1 us (7%)
  matrix products  50.5 us (5%)
  local copies, waits for them, and re-layouts  29.2 us (3%)
  between operations  19.9 us (2%)
    all_gather x2, waiting for transfers between devices, on_device(): correlation = jnp.sum(lax.all_gather(local_correlation, 'batch'), axis=0)  215 us
    all_gather x1, waiting for transfers between devices, on_device(): lax.all_gather(bases, 'batch', axis=1, tiled=True)  166 us
    another operation x29, other arithmetic, on_device(): factor = jnp.linalg.cholesky(correlation)  158 us
    psum x1, waiting for transfers between devices, on_device(): gram_rows = lax.psum(partial_value, 'rows')  109 us
    reduce_scatter x1, waiting for transfers between devices, on_device(): lax.psum_scatter(jnp.dot(bases, q_low, preferred_element_type=jnp.float32...  96.7 us
    another operation x5, other arithmetic, on_device(): q_own = jax.scipy.linalg.solve_triangular(factor, lifted.T, lower=True).T  80.9 us
    psum x1, blocking collectives, on_device(): lax.psum(jnp.sum(jnp.square(bases.astype(jnp.float32))), ('rows', 'batch'))  78.1 us
    all_gather x2, waiting for transfers between devices, on_device(): q_full = lax.all_gather(q_own, 'batch', axis=0, tiled=True)  69.5 us
  transfers between devices with their start and end apart: 7, of which 6 were waited for; matrix products, arithmetic and copies ran while one was open for 1% of the time, Pallas kernels for 0%

profile of v1, /device:TPU:0, one launch (start us, length us, event | category | flops | bytes accessed | tf_op | source)
XLA Modules:
  0.0 1091.0 jit_solution(9517130713374095499)
XLA Ops:
  8.1 166.4 %all-gather.8.cloned.1.call-done = bf16[3072,2048]{1,0:T(8,128)(2,1)} async-done(((bf16[3072,256]{1,0:T(8,128)(2,1)}), bf16[3072,2048]{1,0:T(8,128)(2,1)}) %all-gather.8.cloned.1.call-update) | async-done | bytes 12582928 | tf_op jit(solution)/shard_map/all_gather | solution.py:21
  183.7 78.1 %psum.15 = f32[]{:T(128)} all-reduce(f32[]{:T(128)} %multiply_reduce_fusion), channel_id=1, replica_groups=mesh['rows'=16,'batch'=8] {'rows','batch'}, use_global_device_ids=true, to_apply=%region_2.0 | all-reduce | flops 1 | bytes 8 | tf_op jit(solution)/shard_map/psum | solution.py:19
  262.5 108.8 %all-reduce.3.cloned.1.call-done = f32[256,2048]{1,0:T(8,128)} async-done(((f32[256,2048]{1,0:T(8,128)}), f32[256,2048]{1,0:T(8,128)}) %all-reduce.3.cloned.1.call-update) | async-done | bytes 2097168 | tf_op jit(solution)/shard_map/psum | solution.py:22
  380.1 109.1 %all-gather.14.cloned.1.call-done = f32[4096,512]{1,0:T(8,128)} async-done(((f32[512,512]{1,0:T(8,128)}), f32[4096,512]{1,0:T(8,128)}) %all-gather.14.cloned.1.call-update) | async-done | bytes 8388624 | tf_op jit(solution)/shard_map/all_gather | solution.py:30
  497.4 11.7 %cholesky.286 = f32[128,128]{1,0:T(8,128)S(1)} custom-call(f32[128,128]{1,0:T(8,128)S(1)} %cholesky.426), custom_call_target="Cholesky" | custom-call | tf_op jit(solution)/shard_map/jit(cholesky)/cholesky | solution.py:31
  509.2 9.8 custom-call.27
  521.6 11.8 %cholesky.305 = f32[128,128]{1,0:T(8,128)S(1)} custom-call(f32[128,128]{1,0:T(8,128)S(1)} %cholesky.430), custom_call_target="Cholesky" | custom-call | tf_op jit(solution)/shard_map/jit(cholesky)/cholesky | solution.py:31
  533.4 9.8 custom-call.28
  544.8 11.7 %cholesky.326 = f32[128,128]{1,0:T(8,128)S(1)} custom-call(f32[128,128]{1,0:T(8,128)S(1)} %cholesky.435), custom_call_target="Cholesky" | custom-call | tf_op jit(solution)/shard_map/jit(cholesky)/cholesky | solution.py:31
  557.3 9.8 custom-call.29
  568.5 11.9 %cholesky.343 = f32[128,128]{1,0:T(8,128)S(1)} custom-call(f32[128,128]{1,0:T(8,128)S(1)} %convolution_subtract_fusion.11), custom_call_target="Cholesky" | custom-call | tf_op jit(solution)/shard_map/jit(cholesky)/cholesky | solution.py:31
  585.4 11.5 %while.4 = (s32[]{:T(128)}, f32[512,512]{1,0:T(8,128)}, s32[4,2]{0,1:T(2,128)S(1)}, f32[4,128,128]{2,1,0:T(8,128)S(1)}, s32[]{:T(128)}) while((s32[]{:T(128)}, f32[512,512]{1,0:T(8,128)}, s32[4,2]{0,1:T(2,128)S(1)}, f32[4,128,128]{2,1,0:T(8,128)S(1)}, s32[]{:T(128)}) %tuple.52), condition=%wide.while_cond, body=%wide.while_body.sunk | while | flops 2 | bytes 131181 | solution.py:32
  596.9 39.3 %custom-call.30 = f32[4,128,128]{1,2,0:T(8,128)S(1)} custom-call(f32[4,128,128]{2,1,0:T(8,128)S(1)} %get-tuple-element.21), custom_call_target="InvertDiagBlocksLowerTriangular" | custom-call | tf_op jit(solution)/shard_map/jit(_solve_triangular)/triangular_solve | solution.py:32
  643.2 69.4 %all-gather.12.cloned.1.call-done = f32[2048,512]{1,0:T(8,128)} async-done(((f32[256,512]{1,0:T(8,128)}), f32[2048,512]{1,0:T(8,128)}) %all-gather.12.cloned.1.call-update) | async-done | bytes 4194320 | tf_op jit(solution)/shard_map/all_gather | solution.py:25
  721.5 105.9 %all-gather.16.cloned.1.call-done = f32[4096,512]{1,0:T(8,128)} async-done(((f32[512,512]{1,0:T(8,128)}), f32[4096,512]{1,0:T(8,128)}) %all-gather.16.cloned.1.call-update) | async-done | bytes 8388624 | tf_op jit(solution)/shard_map/all_gather | solution.py:30
  835.7 11.7 %cholesky.358 = f32[128,128]{1,0:T(8,128)S(1)} custom-call(f32[128,128]{1,0:T(8,128)S(1)} %cholesky.439), custom_call_target="Cholesky" | custom-call | tf_op jit(solution)/shard_map/jit(cholesky)/cholesky | solution.py:31
  847.5 9.8 custom-call.31
  859.9 11.9 %cholesky.377 = f32[128,128]{1,0:T(8,128)S(1)} custom-call(f32[128,128]{1,0:T(8,128)S(1)} %cholesky.443), custom_call_target="Cholesky" | custom-call | tf_op jit(solution)/shard_map/jit(cholesky)/cholesky | solution.py:31
  884.5 11.7 %cholesky.398 = f32[128,128]{1,0:T(8,128)S(1)} custom-call(f32[128,128]{1,0:T(8,128)S(1)} %cholesky.448), custom_call_target="Cholesky" | custom-call | tf_op jit(solution)/shard_map/jit(cholesky)/cholesky | solution.py:31
  896.9 9.8 custom-call.33
  908.2 11.9 %cholesky.415 = f32[128,128]{1,0:T(8,128)S(1)} custom-call(f32[128,128]{1,0:T(8,128)S(1)} %convolution_subtract_fusion.10), custom_call_target="Cholesky" | custom-call | tf_op jit(solution)/shard_map/jit(cholesky)/cholesky | solution.py:31
  924.6 11.7 %while.5 = (s32[]{:T(128)}, f32[512,512]{1,0:T(8,128)}, s32[4,2]{0,1:T(2,128)S(1)}, f32[4,128,128]{2,1,0:T(8,128)S(1)}, s32[]{:T(128)}) while((s32[]{:T(128)}, f32[512,512]{1,0:T(8,128)}, s32[4,2]{0,1:T(2,128)S(1)}, f32[4,128,128]{2,1,0:T(8,128)S(1)}, s32[]{:T(128)}) %tuple.72), condition=%wide.while_cond.clone, body=%wide.while_body.clone.sunk | while | flops 2 | bytes 131181 | solution.py:32
  936.3 39.3 %custom-call.34 = f32[4,128,128]{1,2,0:T(8,128)S(1)} custom-call(f32[4,128,128]{2,1,0:T(8,128)S(1)} %get-tuple-element.22), custom_call_target="InvertDiagBlocksLowerTriangular" | custom-call | tf_op jit(solution)/shard_map/jit(_solve_triangular)/triangular_solve | solution.py:32
  985.1 96.7 %reduce-scatter.2.cloned.1.call-done = f32[384,512]{0,1:T(8,128)} async-done(((f32[3072,512]{0,1:T(8,128)}), f32[384,512]{0,1:T(8,128)}) %reduce-scatter.2.cloned.1.call-update) | async-done | bytes 786448 | tf_op jit(solution)/shard_map/reduce_scatter | solution.py:34
  (122 shorter events, 114.7 us)
Async XLA Ops:
  6.5 167.9 %copy-start = (bf16[3072,256]{1,0:T(8,128)(2,1)S(1)}, bf16[3072,256]{1,0:T(8,128)(2,1)}, u32[]{:S(2)}) copy-start(bf16[3072,256]{1,0:T(8,128)(2,1)} %param.5) | copy-start | bytes 4718596
  6.5 167.9 %all-gather.8.cloned.1.call-start = ((), (), s32[]{:S(2)}) async-start(), calls=%async_computation.1 | async-start | bytes 14155776 | tf_op jit(solution)/shard_map/all_gather | solution.py:21
  7.3 255.2 %all-gather.10.cloned.1.call-start = ((), (), s32[]{:S(2)}) async-start(), calls=%async_computation.3 | async-start | bytes 4718592 | tf_op jit(solution)/shard_map/all_gather | solution.py:25
  8.0 363.2 %all-reduce.3.cloned.1.call-start = ((), (), s32[]{:S(2)}) async-start(), calls=%async_computation.2 | async-start | bytes 4194304 | tf_op jit(solution)/shard_map/psum | solution.py:22
  182.2 189.0 %copy-start.3 = (f32[256,512]{1,0:T(8,128)S(1)}, f32[256,512]{1,0:T(8,128)}, u32[]{:S(2)}) copy-start(f32[256,512]{1,0:T(8,128)} %param.6) | copy-start | bytes 1572868
  182.3 306.9 %all-gather.14.cloned.1.call-start = ((), (), s32[]{:S(2)}) async-start(), calls=%async_computation.6 | async-start | bytes 9437184 | tf_op jit(solution)/shard_map/all_gather | solution.py:30
  379.5 333.1 %all-gather.12.cloned.1.call-start = ((), (), s32[]{:S(2)}) async-start(), calls=%async_computation.4 | async-start | bytes 4718592 | tf_op jit(solution)/shard_map/all_gather | solution.py:25
  496.4 1.0 copy-start.2
  643.1 184.3 %all-gather.16.cloned.1.call-start = ((), (), s32[]{:S(2)}) async-start(), calls=%async_computation.7 | async-start | bytes 9437184 | tf_op jit(solution)/shard_map/all_gather | solution.py:30
  721.1 360.7 %reduce-scatter.2.cloned.1.call-start = ((), (), s32[]{:S(2)}) async-start(), calls=%async_computation.5 | async-start | bytes 7077888 | tf_op jit(solution)/shard_map/reduce_scatter | solution.py:34
  834.7 1.0 copy-start.1
Sparse Core Ops, SparseCore 0:
  9.5 164.8 all-gather.7
  176.7 70.8 all-gather.9
  250.1 121.0 all-reduce.2
  379.7 109.4 all-gather.13
  643.2 69.3 all-gather.11
  721.2 106.1 all-gather.15
  985.2 96.5 reduce-scatter.1
